TPU v7x, 256 devices: a whole 4x4x8 slice. The times are simulated.
256 devices in a mesh: lon: 32 (over z, x_lo, core), obs: 8 (over x_hi, y).
Axes of the slice: x: 4 (x_hi: 2, x_lo: 2; x = x_hi * 2 + x_lo), y: 4, z: 8, core: 2. Of those that a mesh axis runs over, the one named last changes fastest.
Arguments:
- perturb: float32 [32768, 1024], P('lon'), may hold values from -6 to 6
- observed: bfloat16 [32768, 1024], P(('lon', 'obs')), may hold values from -6 to 6
- solved: bfloat16 [32768, 1024], P(('lon', 'obs')), may hold values from -6 to 6
- taper_index: int32 [32768, 7168], P('lon', 'obs'), may hold values from 0 to 15
- taper_table: float32 [16], replicated, may hold values from 0.05 to 1
Outputs:
- analysis: float32 [32768, 1024], P(('lon', 'obs'))
All inputs are finite; a program needn't handle non-finite values.
Results may differ from a plain program's by a relative error of at most 0.0035.
Values may be sent and summed in bfloat16 or wider, within the bound.
A program may use at most 128 MiB of HBM per device.

v0:
```python
import jax
import jax.numpy as jnp
from jax import lax
from jax.sharding import Mesh
from jax.sharding import PartitionSpec as P

REACH = 3
OBS = ("obs_0", "obs_1")
LON_OBS = ("lon", "obs_0", "obs_1")


def shifted(value, axis, steps):
    count = lax.axis_size(axis)
    pairs = [(source, (source + steps) % count) for source in range(count)]
    return lax.ppermute(value, axis, pairs)


def sum_in_order(pieces, axes, order):
    inside = pieces.shape[1:]
    pieces = pieces.reshape(*(lax.axis_size(a) for a in axes), *inside)
    pieces = jnp.moveaxis(pieces, order, range(len(axes))).reshape(-1, *inside)
    for k in order:
        pieces = lax.psum_scatter(pieces, axes[k], scatter_dimension=0, tiled=True)
    return pieces[0]


def split_up(shard, dim, length):
    dims = shard.shape
    pieces = shard.reshape(*dims[:dim], length, dims[dim] // length, *dims[dim + 1 :])
    return jnp.moveaxis(pieces, dim, 0)


def sum_by_axis(shard, axes, order, dim):
    length = lax.axis_size(axes)
    return sum_in_order(split_up(shard, dim, length), axes, order)


def block_term(x_half, pair, index_block, taper_table):
    cov = lax.dot_general(
        x_half, pair[0], (((1,), (1,)), ((), ())), preferred_element_type=jnp.float32
    )
    cov = cov / (x_half.shape[1] - 1)
    rho = jnp.zeros(index_block.shape, jnp.float32)
    for level in range(taper_table.shape[0]):
        rho = jnp.where(index_block == level, taper_table[level], rho)
    weighted = (rho * cov).astype(jnp.bfloat16)
    return jnp.dot(weighted, pair[1], preferred_element_type=jnp.float32)


def per_device(perturb, observed, solved, taper_index, taper_table):
    reach = REACH
    width = observed.shape[0]
    x_half = perturb.astype(jnp.bfloat16)

    def index_of(offset):
        return taper_index[:, offset * width : (offset + 1) * width]

    total = block_term(x_half, (observed, solved), index_of(reach), taper_table)
    for moved in list(range(1, reach + 1)) + list(range(-reach, 0)):
        came = shifted((observed, solved), "lon", moved)
        total = total + block_term(x_half, came, index_of(reach - moved), taper_table)
    share = perturb.shape[0] // lax.axis_size(OBS)
    start = lax.axis_index(OBS) * share
    mine = sum_by_axis(total, OBS, (1, 0), 0)
    return lax.dynamic_slice_in_dim(perturb, start, share, 0) + mine


def solution(mesh):
    torus = Mesh(mesh.devices.reshape(mesh.shape["lon"], 2, 4), ("lon", "obs_0", "obs_1"))
    in_specs = (P("lon", None), P(LON_OBS, None), P(LON_OBS, None), P("lon", OBS), P())
    out_specs = P(LON_OBS, None)
    return jax.shard_map(
        per_device, mesh=torus, in_specs=in_specs, out_specs=out_specs, check_vma=False
    )
```

profile of v0, /device:TPU:1, one launch (start us, length us, event | category | flops | bytes accessed | tf_op | source)
XLA Modules:
  0.0 236.8 jit_solution(5451650312064859810)
XLA Ops:
  6.5 0.0 copy-start
  6.5 0.0 copy-start.1
  6.5 0.0 reduce-scatter.3.cloned.1.call-start
  6.5 7.9 %collective-permute-start.6 = (bf16[128,1024]{1,0:T(8,128)(2,1)}, bf16[128,1024]{1,0:T(8,128)(2,1)}, u32[]{:S(2)}, u32[]{:S(2)}) collective-permute-start(bf16[128,1024]{1,0:T(8,128)(2,1)} %param.6), channel_id=1, source_target_pairs={{0,232},{8,240},{16,248},{24,0},{32,8},{40,16},{48,24},{56,32},{64... | collective-permute-start | bytes 786440 | tf_op jit(solution)/shard_map/ppermute | solution.py:15
  14.4 0.0 collective-permute-start.4
  14.4 0.0 collective-permute-start.2
  14.4 3.6 %collective-permute-start.8 = (bf16[128,1024]{1,0:T(8,128)(2,1)}, bf16[128,1024]{1,0:T(8,128)(2,1)S(1)}, u32[]{:S(2)}, u32[]{:S(2)}) collective-permute-start(bf16[128,1024]{1,0:T(8,128)(2,1)} %param.6), channel_id=1, source_target_pairs={{0,240},{8,248},{16,0},{24,8},{32,16},{40,24},{48,32},{56,40},{64,... | collective-permute-start | bytes 786440 | tf_op jit(solution)/shard_map/ppermute | solution.py:15
  18.0 0.3 collective-permute-start.9
  18.3 2.0 fusion.616
  20.2 2.5 %convert_element_type.24 = bf16[1024,1024]{1,0:T(8,128)(2,1)S(1)} convert(f32[1024,1024]{1,0:T(8,128)} %param.5) | non-fusion elementwise | flops 1048576 | bytes 6291456 | tf_op jit(solution)/shard_map/convert_element_type | solution.py:53
  22.8 0.0 copy-done
  22.8 0.0 copy-done.1
  22.8 15.3 %fusion.20 = f32[1024,1024]{1,0:T(8,128)} fusion(bf16[128,1024]{1,0:T(8,128)(2,1)S(1)} %copy-done.1, bf16[1024,1024]{1,0:T(8,128)(2,1)S(1)} %convert_element_type.24, bf16[128,1024]{1,0:T(8,128)(2,1)S(1)} %copy-done, s32[1024,896]{1,0:T(8,128)} %param.8, f32[]{:T(128)} %bitcast.15, f32[]{:T(128)} %bitcast.14, f32[]{:T(128)} %bitcast.13, f32[]{:T(128)} %bitcast.12, ...), kind=kOutput, calls=%fused_computation.28 | convolution fusion | flops 541458432 | bytes 7348224 | tf_op jit(solution)/shard_map/dot_general | solution.py:47
  38.1 0.0 collective-permute-done.8
  38.1 2.0 collective-permute-start
  40.1 0.0 collective-permute-done.9
  40.1 0.1 collective-permute-start.7
  40.2 15.4 %fusion.15 = f32[1024,1024]{1,0:T(8,128)} fusion(bf16[128,1024]{1,0:T(8,128)(2,1)} %collective-permute-done.9, bf16[1024,1024]{1,0:T(8,128)(2,1)S(1)} %convert_element_type.24, bf16[128,1024]{1,0:T(8,128)(2,1)S(1)} %collective-permute-done.8, s32[1024,896]{1,0:T(8,128)} %param.8, f32[]{:T(128)} %bitcast.15, f32[]{:T(128)} %bitcast.14, f32[]{:T(128)} %bitcast.13, ...), kind=kOutput, calls=%fused_computation.23 | convolution fusion | flops 541458432 | bytes 7348224 | tf_op jit(solution)/shard_map/dot_general | solution.py:47
  55.6 0.0 collective-permute-done.6
  55.6 0.6 collective-permute-start.10
  56.2 0.0 collective-permute-done.7
  56.2 2.6 %collective-permute-start.5 = (bf16[128,1024]{1,0:T(8,128)(2,1)S(1)}, bf16[128,1024]{1,0:T(8,128)(2,1)}, u32[]{:S(2)}, u32[]{:S(2)}) collective-permute-start(bf16[128,1024]{1,0:T(8,128)(2,1)S(1)} %copy-done.1), channel_id=1, source_target_pairs={{0,24},{8,32},{16,40},{24,48},{32,56},{40,64},{48,72},{56,80},{64,... | collective-permute-start | bytes 786440 | tf_op jit(solution)/shard_map/ppermute | solution.py:15
  58.8 15.5 %fusion.16 = f32[1024,1024]{1,0:T(8,128)} fusion(bf16[128,1024]{1,0:T(8,128)(2,1)} %collective-permute-done.7, bf16[1024,1024]{1,0:T(8,128)(2,1)S(1)} %convert_element_type.24, bf16[128,1024]{1,0:T(8,128)(2,1)} %collective-permute-done.6, s32[1024,896]{1,0:T(8,128)} %param.8, f32[]{:T(128)} %bitcast.15, f32[]{:T(128)} %bitcast.14, f32[]{:T(128)} %bitcast.13, ...), kind=kOutput, calls=%fused_computation.24 | convolution fusion | flops 541458432 | bytes 7348224 | tf_op jit(solution)/shard_map/dot_general | solution.py:47
  74.3 0.0 collective-permute-done.4
  74.3 1.2 collective-permute-start.3
  75.5 0.0 collective-permute-done.5
  75.5 0.2 collective-permute-start.1
  75.8 15.4 %fusion.17 = f32[1024,1024]{1,0:T(8,128)} fusion(bf16[128,1024]{1,0:T(8,128)(2,1)} %collective-permute-done.5, bf16[1024,1024]{1,0:T(8,128)(2,1)S(1)} %convert_element_type.24, bf16[128,1024]{1,0:T(8,128)(2,1)S(1)} %collective-permute-done.4, s32[1024,896]{1,0:T(8,128)} %param.8, f32[]{:T(128)} %bitcast.15, f32[]{:T(128)} %bitcast.14, f32[]{:T(128)} %bitcast.13, ...), kind=kOutput, calls=%fused_computation.25 | convolution fusion | flops 541458432 | bytes 7348224 | tf_op jit(solution)/shard_map/dot_general | solution.py:47
  91.2 0.0 collective-permute-done.2
  91.2 0.3 collective-permute-start.11
  91.5 0.0 collective-permute-done.3
  91.5 15.4 %fusion.18 = f32[1024,1024]{1,0:T(8,128)} fusion(bf16[128,1024]{1,0:T(8,128)(2,1)} %collective-permute-done.3, bf16[1024,1024]{1,0:T(8,128)(2,1)S(1)} %convert_element_type.24, bf16[128,1024]{1,0:T(8,128)(2,1)S(1)} %collective-permute-done.2, s32[1024,896]{1,0:T(8,128)} %param.8, f32[]{:T(128)} %bitcast.15, f32[]{:T(128)} %bitcast.14, f32[]{:T(128)} %bitcast.13, ...), kind=kOutput, calls=%fused_computation.26 | convolution fusion | flops 541458432 | bytes 7348224 | tf_op jit(solution)/shard_map/dot_general | solution.py:47
  106.8 0.0 collective-permute-done
  106.9 0.0 collective-permute-done.1
  106.9 15.5 %fusion.19 = f32[1024,1024]{1,0:T(8,128)} fusion(bf16[128,1024]{1,0:T(8,128)(2,1)} %collective-permute-done.1, bf16[1024,1024]{1,0:T(8,128)(2,1)S(1)} %convert_element_type.24, bf16[128,1024]{1,0:T(8,128)(2,1)} %collective-permute-done, s32[1024,896]{1,0:T(8,128)} %param.8, f32[]{:T(128)} %bitcast.15, f32[]{:T(128)} %bitcast.14, f32[]{:T(128)} %bitcast.13, ...), kind=kOutput, calls=%fused_computation.27 | convolution fusion | flops 541458432 | bytes 7348224 | tf_op jit(solution)/shard_map/dot_general | solution.py:47
  122.3 0.0 collective-permute-done.10
  122.3 0.0 collective-permute-done.11
  122.3 22.1 %add_add_fusion = f32[1024,1024]{1,0:T(8,128)} fusion(f32[1024,1024]{1,0:T(8,128)} %fusion.15, f32[1024,1024]{1,0:T(8,128)} %fusion.16, f32[1024,1024]{1,0:T(8,128)} %fusion.17, f32[1024,1024]{1,0:T(8,128)} %fusion.18, f32[1024,1024]{1,0:T(8,128)} %fusion.20, f32[1024,1024]{1,0:T(8,128)} %fusion.19, bf16[128,1024]{1,0:T(8,128)(2,1)S(1)} %collective-permute-done.11, ...), kind=kOutput, calls=%fused_computation | convolution fusion | flops 547749888 | bytes 32514048 | tf_op jit(solution)/shard_map/dot_general | solution.py:47
  144.4 4.7 %copy.6 = f32[4,2,128,1024]{3,2,1,0:T(8,128)} copy(f32[4,2,128,1024]{3,2,0,1:T(8,128)} %bitcast.43) | data formatting | bytes 8388608 | tf_op jit(solution)/shard_map/transpose | solution.py:21
  149.1 0.0 reduce-scatter.3.cloned.1.call-update
  149.2 0.0 reduce-scatter.5.cloned.1.call-start
  149.2 49.6 %reduce-scatter.3.cloned.1.call-done = f32[2,128,1024]{2,1,0:T(8,128)} async-done(((f32[8,128,1024]{2,1,0:T(8,128)}), f32[2,128,1024]{2,1,0:T(8,128)}) %reduce-scatter.3.cloned.1.call-update) | async-done | bytes 1048592 | tf_op jit(solution)/shard_map/reduce_scatter | solution.py:23
  198.8 0.0 reduce-scatter.5.cloned.1.call-update
  198.8 29.1 %reduce-scatter.5.cloned.1.call-done = f32[1,128,1024]{2,1,0:T(8,128)} async-done(((f32[2,128,1024]{2,1,0:T(8,128)}), f32[1,128,1024]{2,1,0:T(8,128)}) %reduce-scatter.5.cloned.1.call-update) | async-done | bytes 524304 | tf_op jit(solution)/shard_map/reduce_scatter | solution.py:23
  227.9 2.1 bitcast_add_fusion
Async XLA Ops:
  6.5 16.2 %copy-start = (bf16[128,1024]{1,0:T(8,128)(2,1)S(1)}, bf16[128,1024]{1,0:T(8,128)(2,1)}, u32[]{:S(2)}) copy-start(bf16[128,1024]{1,0:T(8,128)(2,1)} %param.6) | copy-start | bytes 786436
  6.5 16.2 %copy-start.1 = (bf16[128,1024]{1,0:T(8,128)(2,1)S(1)}, bf16[128,1024]{1,0:T(8,128)(2,1)}, u32[]{:S(2)}) copy-start(bf16[128,1024]{1,0:T(8,128)(2,1)} %param.7) | copy-start | bytes 786436
  6.5 192.2 %reduce-scatter.3.cloned.1.call-start = ((), (), s32[]{:S(2)}) async-start(), calls=%async_computation.2 | async-start | bytes 5242880 | tf_op jit(solution)/shard_map/reduce_scatter | solution.py:23
  6.5 49.1 %collective-permute-start.6 = (bf16[128,1024]{1,0:T(8,128)(2,1)}, bf16[128,1024]{1,0:T(8,128)(2,1)}, u32[]{:S(2)}, u32[]{:S(2)}) collective-permute-start(bf16[128,1024]{1,0:T(8,128)(2,1)} %param.6), channel_id=1, source_target_pairs={{0,232},{8,240},{16,248},{24,0},{32,8},{40,16},{48,24},{56,32},{64... | collective-permute-start | bytes 786440 | tf_op jit(solution)/shard_map/ppermute | solution.py:15
  14.4 59.9 %collective-permute-start.4 = (bf16[128,1024]{1,0:T(8,128)(2,1)}, bf16[128,1024]{1,0:T(8,128)(2,1)S(1)}, u32[]{:S(2)}, u32[]{:S(2)}) collective-permute-start(bf16[128,1024]{1,0:T(8,128)(2,1)} %param.6), channel_id=1, source_target_pairs={{0,24},{8,32},{16,40},{24,48},{32,56},{40,64},{48,72},{56,80},{64,... | collective-permute-start | bytes 786440 | tf_op jit(solution)/shard_map/ppermute | solution.py:15
  14.4 76.7 %collective-permute-start.2 = (bf16[128,1024]{1,0:T(8,128)(2,1)}, bf16[128,1024]{1,0:T(8,128)(2,1)S(1)}, u32[]{:S(2)}, u32[]{:S(2)}) collective-permute-start(bf16[128,1024]{1,0:T(8,128)(2,1)} %param.6), channel_id=1, source_target_pairs={{0,16},{8,24},{16,32},{24,40},{32,48},{40,56},{48,64},{56,72},{64,... | collective-permute-start | bytes 786440 | tf_op jit(solution)/shard_map/ppermute | solution.py:15
  14.4 23.7 %collective-permute-start.8 = (bf16[128,1024]{1,0:T(8,128)(2,1)}, bf16[128,1024]{1,0:T(8,128)(2,1)S(1)}, u32[]{:S(2)}, u32[]{:S(2)}) collective-permute-start(bf16[128,1024]{1,0:T(8,128)(2,1)} %param.6), channel_id=1, source_target_pairs={{0,240},{8,248},{16,0},{24,8},{32,16},{40,24},{48,32},{56,40},{64,... | collective-permute-start | bytes 786440 | tf_op jit(solution)/shard_map/ppermute | solution.py:15
  18.0 22.1 %collective-permute-start.9 = (bf16[128,1024]{1,0:T(8,128)(2,1)}, bf16[128,1024]{1,0:T(8,128)(2,1)}, u32[]{:S(2)}, u32[]{:S(2)}) collective-permute-start(bf16[128,1024]{1,0:T(8,128)(2,1)} %param.7), channel_id=1, source_target_pairs={{0,240},{8,248},{16,0},{24,8},{32,16},{40,24},{48,32},{56,40},{64,... | collective-permute-start | bytes 786440 | tf_op jit(solution)/shard_map/ppermute | solution.py:15
  38.1 68.8 %collective-permute-start = (bf16[128,1024]{1,0:T(8,128)(2,1)S(1)}, bf16[128,1024]{1,0:T(8,128)(2,1)}, u32[]{:S(2)}, u32[]{:S(2)}) collective-permute-start(bf16[128,1024]{1,0:T(8,128)(2,1)S(1)} %copy-done), channel_id=1, source_target_pairs={{0,8},{8,16},{16,24},{24,32},{32,40},{40,48},{48,56},{56,64},{64,7... | collective-permute-start | bytes 786440 | tf_op jit(solution)/shard_map/ppermute | solution.py:15
  40.1 16.1 %collective-permute-start.7 = (bf16[128,1024]{1,0:T(8,128)(2,1)S(1)}, bf16[128,1024]{1,0:T(8,128)(2,1)}, u32[]{:S(2)}, u32[]{:S(2)}) collective-permute-start(bf16[128,1024]{1,0:T(8,128)(2,1)S(1)} %copy-done.1), channel_id=1, source_target_pairs={{0,232},{8,240},{16,248},{24,0},{32,8},{40,16},{48,24},{56,32},{64... | collective-permute-start | bytes 786440 | tf_op jit(solution)/shard_map/ppermute | solution.py:15
  55.6 66.7 %collective-permute-start.10 = (bf16[128,1024]{1,0:T(8,128)(2,1)S(1)}, bf16[128,1024]{1,0:T(8,128)(2,1)S(1)}, u32[]{:S(2)}, u32[]{:S(2)}) collective-permute-start(bf16[128,1024]{1,0:T(8,128)(2,1)S(1)} %copy-done), channel_id=1, source_target_pairs={{0,248},{8,0},{16,8},{24,16},{32,24},{40,32},{48,40},{56,48},{64,5... | collective-permute-start | bytes 786440 | tf_op jit(solution)/shard_map/ppermute | solution.py:15
  56.2 19.3 %collective-permute-start.5 = (bf16[128,1024]{1,0:T(8,128)(2,1)S(1)}, bf16[128,1024]{1,0:T(8,128)(2,1)}, u32[]{:S(2)}, u32[]{:S(2)}) collective-permute-start(bf16[128,1024]{1,0:T(8,128)(2,1)S(1)} %copy-done.1), channel_id=1, source_target_pairs={{0,24},{8,32},{16,40},{24,48},{32,56},{40,64},{48,72},{56,80},{64,... | collective-permute-start | bytes 786440 | tf_op jit(solution)/shard_map/ppermute | solution.py:15
  74.3 17.2 %collective-permute-start.3 = (bf16[128,1024]{1,0:T(8,128)(2,1)S(1)}, bf16[128,1024]{1,0:T(8,128)(2,1)}, u32[]{:S(2)}, u32[]{:S(2)}) collective-permute-start(bf16[128,1024]{1,0:T(8,128)(2,1)S(1)} %copy-done.1), channel_id=1, source_target_pairs={{0,16},{8,24},{16,32},{24,40},{32,48},{40,56},{48,64},{56,72},{64,... | collective-permute-start | bytes 786440 | tf_op jit(solution)/shard_map/ppermute | solution.py:15
  75.5 31.3 %collective-permute-start.1 = (bf16[128,1024]{1,0:T(8,128)(2,1)S(1)}, bf16[128,1024]{1,0:T(8,128)(2,1)}, u32[]{:S(2)}, u32[]{:S(2)}) collective-permute-start(bf16[128,1024]{1,0:T(8,128)(2,1)S(1)} %copy-done.1), channel_id=1, source_target_pairs={{0,8},{8,16},{16,24},{24,32},{32,40},{40,48},{48,56},{56,64},{64,7... | collective-permute-start | bytes 786440 | tf_op jit(solution)/shard_map/ppermute | solution.py:15
  91.2 31.1 %collective-permute-start.11 = (bf16[128,1024]{1,0:T(8,128)(2,1)S(1)}, bf16[128,1024]{1,0:T(8,128)(2,1)S(1)}, u32[]{:S(2)}, u32[]{:S(2)}) collective-permute-start(bf16[128,1024]{1,0:T(8,128)(2,1)S(1)} %copy-done.1), channel_id=1, source_target_pairs={{0,248},{8,0},{16,8},{24,16},{32,24},{40,32},{48,40},{56,48},{64,5... | collective-permute-start | bytes 786440 | tf_op jit(solution)/shard_map/ppermute | solution.py:15
  149.2 78.8 %reduce-scatter.5.cloned.1.call-start = ((), (), s32[]{:S(2)}) async-start(), calls=%async_computation.3 | async-start | bytes 1572864 | tf_op jit(solution)/shard_map/reduce_scatter | solution.py:23
Sparse Core Ops, SparseCore 0:
  149.3 49.4 reduce-scatter.2
  201.3 26.5 reduce-scatter.4
where the time goes:
time: 238 us; the launch traced here: 237 us
  matrix products  114 us (48%)
  waiting for transfers between devices  78.7 us (33%)
  starting transfers between devices  18.9 us (8%)
  between operations  13.5 us (6%)
  local copies, waits for them, and re-layouts  6.69 us (3%)
  other arithmetic  4.57 us (2%)
    dot_general x7, matrix products, block_term(): return jnp.dot(weighted, pair[1], preferred_element_type=jnp.float32)  114 us
    reduce_scatter x2, waiting for transfers between devices, sum_in_order(): pieces = lax.psum_scatter(pieces, axes[k], scatter_dimension=0, tiled=True)  78.7 us
    ppermute x12, starting transfers between devices, shifted(): return lax.ppermute(value, axis, pairs)  18.9 us
  transfers between devices with their start and end apart: 14, of which 2 were waited for; matrix products, arithmetic and copies ran while one was open for 41% of the time, Pallas kernels for 0%

commit v1 on v0

v1 whole, which is shorter than its diff:
```python
import functools

import jax
import jax.numpy as jnp
from jax import lax
from jax.experimental import pallas as pl
from jax.experimental.pallas import tpu as pltpu
from jax.sharding import Mesh
from jax.sharding import PartitionSpec as P

MESH = pl.DeviceIdType.MESH
BF16, F32 = jnp.bfloat16, jnp.float32
SLOTS = 7
CUTS = 2
PARTS = 4
OUTER = (0, 1, 2, 3, -3, -2, -1)
INNER = (0, -1, 2, 1, 3, -2, -3)


def kernel(
    perturb, observed, solved, taper_index, table, out,
    x_full, x_half, obs, sol, index, rho, weighted, part, passed, joined, came, half_out, half_in, half_own, result,
    load_sem, obs_load_sem, sol_load_sem, index_sem, out_sem,
    obs_send, obs_recv, sol_send, sol_recv, y_send, y_recv, x_send, x_recv,
):
    z, xl, core, xh, y = (lax.axis_index(a) for a in ("z", "xl", "core", "xh", "y"))
    depth, ring = lax.axis_size("z"), lax.axis_size("y")
    rows, members = perturb.shape
    width = observed.shape[0]
    cut = width // CUTS
    span = members // PARTS
    share = rows // (2 * ring)
    way = 1 - 2 * xl
    side = 2 * core - 1
    inner = xl + core - 2 * xl * core

    mate = {"core": 1 - core}
    across = {"xl": 1 - xl}
    slant = {"z": lax.rem(z + side + depth, depth), "core": 1 - core}
    ahead = {"z": lax.rem(z + way + depth, depth)}
    behind = {"z": lax.rem(z - way + depth, depth)}
    y_up, y_down = lax.rem(y + 1, ring), lax.rem(y + ring - 1, ring)
    far = lax.rem(y + 2, ring)
    y_next = (y_up, y_down)
    opposite = {"xh": 1 - xh}

    step = rows // 4
    loads = [
        pltpu.make_async_copy(perturb.at[pl.ds(i * step, step)], x_full.at[pl.ds(i * step, step)], load_sem.at[i])
        for i in range(4)
    ]
    own_obs = pltpu.make_async_copy(observed, obs.at[0], obs_load_sem)
    own_sol = [
        pltpu.make_async_copy(solved.at[:, pl.ds(c * span, span)], sol.at[c, pl.ds(0, width)], sol_load_sem.at[c])
        for c in range(PARTS)
    ]
    index_loads = []
    for slot in range(SLOTS):
        offset = way * (OUTER[slot] + inner * (INNER[slot] - OUTER[slot]))
        start = pl.multiple_of((offset + SLOTS // 2) * width, width)
        index_loads.append(
            pltpu.make_async_copy(taper_index.at[:, pl.ds(start, width)], index.at[slot], index_sem.at[slot])
        )

    barrier = pltpu.get_barrier_semaphore()
    peers = (mate, across, slant, ahead, behind, {"y": y_up}, {"y": y_down}, opposite)
    for peer in peers:
        pl.semaphore_signal(barrier, inc=1, device_id=peer, device_id_type=MESH)
    own_obs.start()
    for i in range(4):
        loads[i].start()
    for slot in (0, 1, 4, 2, 3, 5, 6):
        index_loads[slot].start()
    for c in range(PARTS):
        own_sol[c].start()
    pl.semaphore_wait(barrier, len(peers))

    def remote(src, dst, send, recv, peer):
        return pltpu.make_async_remote_copy(
            src_ref=src, dst_ref=dst, send_sem=send, recv_sem=recv, device_id=peer, device_id_type=MESH
        )

    routes = {1: (0, mate), 2: (0, across), 3: (2, mate), 4: (0, slant), 5: (2, ahead), 6: (5, mate)}

    def obs_copy(slot, i):
        source, peer = routes[slot]
        run = pl.ds(i * cut, cut)
        src = observed.at[run] if source == 0 else obs.at[source, run]
        return remote(src, obs.at[slot, run], obs_send.at[slot, i], obs_recv.at[slot, i], peer)

    def sol_copy(slot, c):
        source, peer = routes[slot]
        src = solved.at[:, pl.ds(c * span, span)] if source == 0 else sol.at[c, pl.ds(source * width, width)]
        return remote(src, sol.at[c, pl.ds(slot * width, width)], sol_send.at[slot, c], sol_recv.at[slot, c], peer)

    obs_copies = {(slot, i): obs_copy(slot, i) for slot in routes for i in range(CUTS)}
    sol_copies = {(slot, c): sol_copy(slot, c) for slot in routes for c in range(PARTS)}

    for i in range(CUTS):
        for slot in (2, 4, 1):
            obs_copies[slot, i].start()
    for c in range(PARTS):
        sol_copies[2, c].start()

    scale = 1.0 / (members - 1)
    levels = [table[i] * scale for i in range(table.shape[0])]

    def find_rho(slot):
        index_loads[slot].wait()

        def body(i, carry):
            run = pl.ds(pl.multiple_of(i * 64, 64), 64)
            at = index[slot, run, :]
            values = levels
            bit = 1
            while len(values) > 1:
                odd = (at & bit) != 0
                values = [jnp.where(odd, values[k + 1], values[k]) for k in range(0, len(values), 2)]
                bit *= 2
            rho[slot, run, :] = values[0]
            return carry

        lax.fori_loop(0, rows // 64, body, 0)

    def weigh(slot):
        block = obs.at[slot]

        def body(i, carry):
            run = pl.ds(pl.multiple_of(i * 256, 256), 256)
            cov = lax.dot_general(
                x_half[run, :], block[...], (((1,), (1,)), ((), ())), preferred_element_type=F32
            )
            weighted[run, slot * width : (slot + 1) * width] = (rho[slot, run, :] * cov).astype(BF16)
            return carry

        lax.fori_loop(0, rows // 256, body, 0)

    def obs_came(slot):
        for i in range(CUTS):
            obs_copies[slot, i].wait_recv()

    for i in range(4):
        loads[i].wait()

        def convert(j, carry):
            run = pl.ds(pl.multiple_of(i * step + j * 16, 16), 16)
            x_half[run, :] = x_full[run, :].astype(BF16)
            return carry

        lax.fori_loop(0, step // 16, convert, 0)
    find_rho(0)
    own_obs.wait()
    weigh(0)
    for i in range(CUTS):
        obs_copies[2, i].wait_recv()
        obs_copies[5, i].start()
        obs_copies[3, i].start()
        if i == 0:
            find_rho(1)
            obs_came(1)
            weigh(1)
            find_rho(4)
    sol_copies[4, 0].start()
    sol_copies[1, 0].start()
    find_rho(2)
    weigh(2)
    obs_came(4)
    weigh(4)
    sol_copies[2, 0].wait_recv()
    sol_copies[5, 0].start()
    sol_copies[3, 0].start()
    find_rho(3)
    find_rho(5)
    obs_copies[5, 0].wait_recv()
    obs_copies[6, 0].start()
    find_rho(6)
    obs_came(3)
    weigh(3)
    for i in range(1, CUTS):
        obs_copies[5, i].wait_recv()
        obs_copies[6, i].start()
    weigh(5)
    for c in range(1, PARTS):
        sol_copies[4, c].start()
        sol_copies[1, c].start()
        sol_copies[2, c].wait_recv()
        sol_copies[5, c].start()
        sol_copies[3, c].start()
    obs_came(6)
    weigh(6)

    def rows_of(half, where):
        return pl.ds(pl.multiple_of((half * ring + where) * share, share), share)

    def y_copy(c, way_y, kind):
        peer = {"y": y_next[way_y]}
        if kind == 0:
            src, dst = part.at[c, rows_of(way_y, far)], passed.at[c, way_y]
        elif kind == 1:
            src, dst = part.at[c, rows_of(1 - way_y, y_next[way_y])], came.at[c, way_y, 1 - way_y]
        else:
            src, dst = joined.at[c, way_y], came.at[c, way_y, way_y]
        return remote(src, dst, y_send.at[c, way_y, kind], y_recv.at[c, way_y, kind], peer)

    y_copies = {(c, w, k): y_copy(c, w, k) for c in range(PARTS) for w in range(2) for k in range(3)}
    x_copies = [
        remote(half_out.at[c], half_in.at[c], x_send.at[c], x_recv.at[c], opposite) for c in range(PARTS)
    ]
    writes = [
        pltpu.make_async_copy(result.at[c], out.at[:, pl.ds(c * span, span)], out_sem.at[c]) for c in range(PARTS)
    ]

    def increments(c):
        def body(i, carry):
            run = pl.ds(pl.multiple_of(i * 256, 256), 256)
            total = jnp.dot(weighted[run, :], sol[c], preferred_element_type=F32)
            part[c, run, :] = total.astype(BF16)
            return carry

        lax.fori_loop(0, rows // 256, body, 0)

    def join(c):
        for w in range(2):
            y_copies[c, w, 0].wait_recv()
            joined[c, w] = (part[c, rows_of(w, y_next[w]), :].astype(F32) + passed[c, w].astype(F32)).astype(BF16)
            y_copies[c, w, 2].start()

    def gather(c):
        for w in range(2):
            for k in (1, 2):
                y_copies[c, w, k].wait_recv()

        def sum_of(half):
            mine = part[c, rows_of(half, y), :].astype(F32)
            return mine + came[c, 0, half].astype(F32) + came[c, 1, half].astype(F32)

        half_out[c] = sum_of(1 - xh).astype(BF16)
        x_copies[c].start()
        half_own[c] = sum_of(xh) + x_full[rows_of(xh, y), c * span : (c + 1) * span]

    def finish(c):
        x_copies[c].wait_recv()
        result[c] = half_own[c] + half_in[c].astype(F32)
        writes[c].start()

    for c in range(PARTS):
        sol_copies[5, c].wait_recv()
        sol_copies[6, c].start()
        own_sol[c].wait()
        for slot in (1, 3, 4, 6):
            sol_copies[slot, c].wait_recv()
        increments(c)
        for k in range(2):
            for w in range(2):
                y_copies[c, w, k].start()
        if c >= 1:
            join(c - 1)
        if c >= 2:
            gather(c - 2)
    join(PARTS - 1)
    for c in range(max(PARTS - 2, 0), PARTS):
        gather(c)
    for c in range(PARTS):
        finish(c)
    for copy in (*obs_copies.values(), *sol_copies.values(), *y_copies.values(), *x_copies):
        copy.wait_send()
    for copy in writes:
        copy.wait()


def per_device(perturb, observed, solved, taper_index, taper_table):
    rows, members = perturb.shape
    width = observed.shape[0]
    ring = lax.axis_size("y")
    share, span = rows // (2 * ring), members // PARTS
    anywhere = pl.BlockSpec(memory_space=pl.ANY)
    dma = pltpu.SemaphoreType.DMA
    return pl.pallas_call(
        kernel,
        out_shape=jax.ShapeDtypeStruct((share, members), F32),
        in_specs=[anywhere] * 4 + [pl.BlockSpec(memory_space=pltpu.SMEM)],
        out_specs=anywhere,
        scratch_shapes=[
            pltpu.VMEM((rows, members), F32),
            pltpu.VMEM((rows, members), BF16),
            pltpu.VMEM((SLOTS, width, members), BF16),
            pltpu.VMEM((PARTS, SLOTS * width, span), BF16),
            pltpu.VMEM((SLOTS, rows, width), jnp.int32),
            pltpu.VMEM((SLOTS, rows, width), F32),
            pltpu.VMEM((rows, SLOTS * width), BF16),
            pltpu.VMEM((PARTS, rows, span), BF16),
            pltpu.VMEM((PARTS, 2, share, span), BF16),
            pltpu.VMEM((PARTS, 2, share, span), BF16),
            pltpu.VMEM((PARTS, 2, 2, share, span), BF16),
            pltpu.VMEM((PARTS, share, span), BF16),
            pltpu.VMEM((PARTS, share, span), BF16),
            pltpu.VMEM((PARTS, share, span), F32),
            pltpu.VMEM((PARTS, share, span), F32),
            dma((4,)),
            dma,
            dma((PARTS,)),
            dma((SLOTS,)),
            dma((PARTS,)),
            dma((SLOTS, CUTS)),
            dma((SLOTS, CUTS)),
            dma((SLOTS, PARTS)),
            dma((SLOTS, PARTS)),
            dma((PARTS, 2, 3)),
            dma((PARTS, 2, 3)),
            dma((PARTS,)),
            dma((PARTS,)),
        ],
        compiler_params=pltpu.CompilerParams(
            collective_id=0, has_side_effects=True, vmem_limit_bytes=48 * 1024 * 1024
        ),
        name="tile_update",
    )(perturb, observed, solved, taper_index, taper_table)


AXES = ("z", "xl", "core", "xh", "y")


def solution(mesh):
    lon, obs = mesh.shape["lon"], mesh.shape["obs"]
    torus = Mesh(mesh.devices.reshape(lon // 4, 2, 2, 2, obs // 2), AXES)
    near, group = AXES[:3], AXES[3:]
    in_specs = (P(near, None), P(AXES, None), P(AXES, None), P(near, group), P())
    return jax.shard_map(
        per_device, mesh=torus, in_specs=in_specs, out_specs=P(AXES, None), check_vma=False
    )
```

time: 238 us -> 60.6 us (0.25)
  matrix products: 114 us -> 0 us
  waiting for transfers between devices: 78.7 us -> 0 us
  Pallas kernels: 0 us -> 55 us
  starting transfers between devices: 18.9 us -> 0 us
  between operations: 13.5 us -> 0.01 us
  other arithmetic: 4.57 us -> 0 us
    dot_general x7 -> x0, matrix products: 114 us -> none  [block_term(): return jnp.dot(weighted, pair[1], preferred_element_type=jnp.float32)]
    reduce_scatter x2 -> x0, waiting for transfers between devices: 78.7 us -> none  [sum_in_order(): pieces = lax.psum_scatter(pieces, axes[k], scatter_dimension=0, tiled=True)]
    pallas_call x0 -> x1, Pallas kernels: none -> 55 us  [per_device(): pl.pallas_call(kernel, out_shape=jax.ShapeDtypeStruct((share, members), F...]
    ppermute x12 -> x0, starting transfers between devices: 18.9 us -> none  [shifted(): return lax.ppermute(value, axis, pairs)]
    unnamed x4 -> x9, local copies, waits for them, and re-layouts: 0.01 us -> 5.39 us
    transpose x1 -> x0, local copies, waits for them, and re-layouts: 4.73 us -> none  [sum_in_order(): pieces = jnp.moveaxis(pieces, order, range(len(axes))).reshape(-1, *inside)]
    convert_element_type x1 -> x0, other arithmetic: 2.51 us -> none  [per_device(): x_half = perturb.astype(jnp.bfloat16)]
  transfers between devices with their start and end apart: 14 -> 0, of which waited for: 2 -> 0; matrix products, arithmetic and copies ran while one was open for 41% -> 0% of each run, Pallas kernels for 0% -> 0%
where the time goes in v1:
time: 60.6 us; the launch traced here: 60.4 us
  Pallas kernels  55 us (91%)
  local copies, waits for them, and re-layouts  5.39 us (9%)
    pallas_call x1, Pallas kernels, per_device(): pl.pallas_call(kernel, out_shape=jax.ShapeDtypeStruct((share, members), F...  55 us
    unnamed x9, local copies, waits for them, and re-layouts  5.39 us

profile of v1, /device:TPU:1, one launch (start us, length us, event | category | flops | bytes accessed | tf_op | source)
XLA Modules:
  0.0 60.4 jit_solution(15563879615094503973)
XLA Ops:
  0.0 0.0 copy-start
  0.0 2.0 %copy-done = s32[1024,896]{1,0:T(8,128)S(1)} copy-done((s32[1024,896]{1,0:T(8,128)S(1)}, s32[1024,896]{1,0:T(8,128)}, u32[]{:S(2)}) %copy-start) | copy-done | bytes 3670040
  2.0 0.0 copy-start.1
  2.0 0.9 %copy-done.1 = bf16[128,1024]{1,0:T(8,128)(2,1)S(1)} copy-done((bf16[128,1024]{1,0:T(8,128)(2,1)S(1)}, bf16[128,1024]{1,0:T(8,128)(2,1)}, u32[]{:S(2)}) %copy-start.1) | copy-done | bytes 262168
  3.0 0.0 copy-start.2
  3.0 0.9 %copy-done.2 = bf16[128,1024]{1,0:T(8,128)(2,1)S(1)} copy-done((bf16[128,1024]{1,0:T(8,128)(2,1)S(1)}, bf16[128,1024]{1,0:T(8,128)(2,1)}, u32[]{:S(2)}) %copy-start.2) | copy-done | bytes 262168
  3.9 0.0 copy-start.3
  3.9 0.7 %copy-done.3 = f32[16]{0:T(128)S(1)} copy-done((f32[16]{0:T(128)S(1)}, f32[16]{0:T(128)}, u32[]{:S(2)}) %copy-start.3) | copy-done | bytes 88
  4.6 55.0 %tile_update.1 = f32[128,1024]{1,0:T(8,128)S(1)} custom-call(f32[1024,1024]{1,0:T(8,128)} %perturb.1, bf16[128,1024]{1,0:T(8,128)(2,1)S(1)} %copy-done.1, bf16[128,1024]{1,0:T(8,128)(2,1)S(1)} %copy-done.2, s32[1024,896]{1,0:T(8,128)S(1)} %copy-done, f32[16]{0:T(128)S(1)} %copy-done.3), custom_call_target="tpu_custom_call" | custom-call | tf_op jit(solution)/shard_map/tile_update/pallas_call | solution.py:278
  59.6 0.8 %copy.7 = f32[128,1024]{1,0:T(8,128)} copy(f32[128,1024]{1,0:T(8,128)S(1)} %tile_update.1) | data formatting | bytes 1048576
Async XLA Ops:
  0.0 2.0 %copy-start = (s32[1024,896]{1,0:T(8,128)S(1)}, s32[1024,896]{1,0:T(8,128)}, u32[]{:S(2)}) copy-start(s32[1024,896]{1,0:T(8,128)} %taper_index.1) | copy-start | bytes 11010052
  2.0 0.9 %copy-start.1 = (bf16[128,1024]{1,0:T(8,128)(2,1)S(1)}, bf16[128,1024]{1,0:T(8,128)(2,1)}, u32[]{:S(2)}) copy-start(bf16[128,1024]{1,0:T(8,128)(2,1)} %observed.1) | copy-start | bytes 786436
  3.0 0.9 %copy-start.2 = (bf16[128,1024]{1,0:T(8,128)(2,1)S(1)}, bf16[128,1024]{1,0:T(8,128)(2,1)}, u32[]{:S(2)}) copy-start(bf16[128,1024]{1,0:T(8,128)(2,1)} %solved.1) | copy-start | bytes 786436
  3.9 0.7 %copy-start.3 = (f32[16]{0:T(128)S(1)}, f32[16]{0:T(128)}, u32[]{:S(2)}) copy-start(f32[16]{0:T(128)} %table.1) | copy-start | bytes 196

commit v2 on v1

--- a/solution.py
+++ b/solution.py
@@ -12,6 +12,7 @@
 BF16, F32 = jnp.bfloat16, jnp.float32
 SLOTS = 7
 CUTS = 2
+TILE = 256
 PARTS = 4
 OUTER = (0, 1, 2, 3, -3, -2, -1)
 INNER = (0, -1, 2, 1, 3, -2, -3)
@@ -49,7 +50,7 @@
         pltpu.make_async_copy(perturb.at[pl.ds(i * step, step)], x_full.at[pl.ds(i * step, step)], load_sem.at[i])
         for i in range(4)
     ]
-    own_obs = pltpu.make_async_copy(observed, obs.at[0], obs_load_sem)
+    own_obs = pltpu.make_async_copy(observed, obs.at[pl.ds(0, width)], obs_load_sem)
     own_sol = [
         pltpu.make_async_copy(solved.at[:, pl.ds(c * span, span)], sol.at[c, pl.ds(0, width)], sol_load_sem.at[c])
         for c in range(PARTS)
@@ -80,13 +81,12 @@
             src_ref=src, dst_ref=dst, send_sem=send, recv_sem=recv, device_id=peer, device_id_type=MESH
         )
 
-    routes = {1: (0, mate), 2: (0, across), 3: (2, mate), 4: (0, slant), 5: (2, ahead), 6: (5, mate)}
+    routes = {1: (0, mate), 2: (0, across), 4: (0, slant), 5: (2, ahead), 3: (2, mate), 6: (5, mate)}
 
     def obs_copy(slot, i):
         source, peer = routes[slot]
-        run = pl.ds(i * cut, cut)
-        src = observed.at[run] if source == 0 else obs.at[source, run]
-        return remote(src, obs.at[slot, run], obs_send.at[slot, i], obs_recv.at[slot, i], peer)
+        src = observed.at[pl.ds(i * cut, cut)] if source == 0 else obs.at[pl.ds(source * width + i * cut, cut)]
+        return remote(src, obs.at[pl.ds(slot * width + i * cut, cut)], obs_send.at[slot, i], obs_recv.at[slot, i], peer)
 
     def sol_copy(slot, c):
         source, peer = routes[slot]
@@ -102,38 +102,29 @@
     for c in range(PARTS):
         sol_copies[2, c].start()
 
-    scale = 1.0 / (members - 1)
-    levels = [table[i] * scale for i in range(table.shape[0])]
-
     def find_rho(slot):
         index_loads[slot].wait()
+        values = jnp.broadcast_to(table[...], (64, width))
 
         def body(i, carry):
             run = pl.ds(pl.multiple_of(i * 64, 64), 64)
-            at = index[slot, run, :]
-            values = levels
-            bit = 1
-            while len(values) > 1:
-                odd = (at & bit) != 0
-                values = [jnp.where(odd, values[k + 1], values[k]) for k in range(0, len(values), 2)]
-                bit *= 2
-            rho[slot, run, :] = values[0]
+            rho[run, slot * width : (slot + 1) * width] = jnp.take_along_axis(values, index[slot, run, :], axis=1)
             return carry
 
         lax.fori_loop(0, rows // 64, body, 0)
 
-    def weigh(slot):
-        block = obs.at[slot]
+    def weigh(first, count):
+        columns = slice(first * width, (first + count) * width)
 
         def body(i, carry):
-            run = pl.ds(pl.multiple_of(i * 256, 256), 256)
+            run = pl.ds(pl.multiple_of(i * TILE, TILE), TILE)
             cov = lax.dot_general(
-                x_half[run, :], block[...], (((1,), (1,)), ((), ())), preferred_element_type=F32
+                x_half[run, :], obs[columns, :], (((1,), (1,)), ((), ())), preferred_element_type=F32
             )
-            weighted[run, slot * width : (slot + 1) * width] = (rho[slot, run, :] * cov).astype(BF16)
+            weighted[run, columns] = (rho[run, columns] * cov).astype(BF16)
             return carry
 
-        lax.fori_loop(0, rows // 256, body, 0)
+        lax.fori_loop(0, rows // TILE, body, 0)
 
     def obs_came(slot):
         for i in range(CUTS):
@@ -148,46 +139,49 @@
             return carry
 
         lax.fori_loop(0, step // 16, convert, 0)
-    find_rho(0)
-    own_obs.wait()
-    weigh(0)
-    for i in range(CUTS):
-        obs_copies[2, i].wait_recv()
-        obs_copies[5, i].start()
-        obs_copies[3, i].start()
-        if i == 0:
-            find_rho(1)
-            obs_came(1)
-            weigh(1)
-            find_rho(4)
-    sol_copies[4, 0].start()
-    sol_copies[1, 0].start()
-    find_rho(2)
-    weigh(2)
-    obs_came(4)
-    weigh(4)
-    sol_copies[2, 0].wait_recv()
-    sol_copies[5, 0].start()
-    sol_copies[3, 0].start()
-    find_rho(3)
-    find_rho(5)
-    obs_copies[5, 0].wait_recv()
-    obs_copies[6, 0].start()
-    find_rho(6)
-    obs_came(3)
-    weigh(3)
-    for i in range(1, CUTS):
-        obs_copies[5, i].wait_recv()
-        obs_copies[6, i].start()
-    weigh(5)
-    for c in range(1, PARTS):
+    def pass_obs(slot_from, i):
+        obs_copies[slot_from, i].wait_recv()
+        for slot, (source, _) in routes.items():
+            if source == slot_from:
+                obs_copies[slot, i].start()
+
+    def send_sol(c):
         sol_copies[4, c].start()
         sol_copies[1, c].start()
-        sol_copies[2, c].wait_recv()
-        sol_copies[5, c].start()
-        sol_copies[3, c].start()
+
+    def pass_sol(slot_from, c):
+        sol_copies[slot_from, c].wait_recv()
+        for slot, (source, _) in routes.items():
+            if source == slot_from:
+                sol_copies[slot, c].start()
+
+    find_rho(0)
+    find_rho(1)
+    own_obs.wait()
+    obs_came(1)
+    weigh(0, 2)
+    pass_obs(2, 0)
+    find_rho(4)
+    obs_came(4)
+    weigh(4, 1)
+    pass_obs(2, 1)
+    send_sol(0)
+    find_rho(2)
+    find_rho(3)
+    obs_came(3)
+    weigh(2, 2)
+    pass_sol(2, 0)
+    send_sol(1)
+    find_rho(5)
+    find_rho(6)
+    pass_obs(5, 0)
+    pass_sol(2, 1)
+    send_sol(2)
+    pass_obs(5, 1)
     obs_came(6)
-    weigh(6)
+    weigh(5, 2)
+    pass_sol(2, 2)
+    send_sol(3)
 
     def rows_of(half, where):
         return pl.ds(pl.multiple_of((half * ring + where) * share, share), share)
@@ -244,8 +238,7 @@
         writes[c].start()
 
     for c in range(PARTS):
-        sol_copies[5, c].wait_recv()
-        sol_copies[6, c].start()
+        pass_sol(5, c)
         own_sol[c].wait()
         for slot in (1, 3, 4, 6):
             sol_copies[slot, c].wait_recv()
@@ -253,6 +246,8 @@
         for k in range(2):
             for w in range(2):
                 y_copies[c, w, k].start()
+        if c == 0:
+            pass_sol(2, 3)
         if c >= 1:
             join(c - 1)
         if c >= 2:
@@ -273,20 +268,22 @@
     width = observed.shape[0]
     ring = lax.axis_size("y")
     share, span = rows // (2 * ring), members // PARTS
+    levels = jnp.pad(taper_table, (0, width - taper_table.shape[0])) / (members - 1)
+    levels = levels.reshape(1, width)
     anywhere = pl.BlockSpec(memory_space=pl.ANY)
     dma = pltpu.SemaphoreType.DMA
     return pl.pallas_call(
         kernel,
         out_shape=jax.ShapeDtypeStruct((share, members), F32),
-        in_specs=[anywhere] * 4 + [pl.BlockSpec(memory_space=pltpu.SMEM)],
+        in_specs=[anywhere] * 4 + [pl.BlockSpec(memory_space=pltpu.VMEM)],
         out_specs=anywhere,
         scratch_shapes=[
             pltpu.VMEM((rows, members), F32),
             pltpu.VMEM((rows, members), BF16),
-            pltpu.VMEM((SLOTS, width, members), BF16),
+            pltpu.VMEM((SLOTS * width, members), BF16),
             pltpu.VMEM((PARTS, SLOTS * width, span), BF16),
             pltpu.VMEM((SLOTS, rows, width), jnp.int32),
-            pltpu.VMEM((SLOTS, rows, width), F32),
+            pltpu.VMEM((rows, SLOTS * width), F32),
             pltpu.VMEM((rows, SLOTS * width), BF16),
             pltpu.VMEM((PARTS, rows, span), BF16),
             pltpu.VMEM((PARTS, 2, share, span), BF16),
@@ -311,10 +308,10 @@
             dma((PARTS,)),
         ],
         compiler_params=pltpu.CompilerParams(
-            collective_id=0, has_side_effects=True, vmem_limit_bytes=48 * 1024 * 1024
+            collective_id=0, has_side_effects=True, vmem_limit_bytes=67_000_000
         ),
         name="tile_update",
-    )(perturb, observed, solved, taper_index, taper_table)
+    )(perturb, observed, solved, taper_index, levels)
 
 
 AXES = ("z", "xl", "core", "xh", "y")

time: 60.6 us -> 58.1 us (0.959)
  local copies, waits for them, and re-layouts: 5.39 us -> 1.89 us
  other arithmetic: 0 us -> 1.17 us
    unnamed x9 -> x1, local copies, waits for them, and re-layouts: 5.39 us -> 1.89 us
    reshape x0 -> x1, other arithmetic: none -> 1.17 us  [per_device(): levels = levels.reshape(1, width)]
where the time goes in v2:
time: 58.1 us; the launch traced here: 57.9 us
  Pallas kernels  54.9 us (94%)
  local copies, waits for them, and re-layouts  1.89 us (3%)
  other arithmetic  1.17 us (2%)
    pallas_call x1, Pallas kernels, per_device(): pl.pallas_call(kernel, out_shape=jax.ShapeDtypeStruct((share, members), F...  54.9 us
    unnamed x1, local copies, waits for them, and re-layouts  1.89 us
    reshape x1, other arithmetic, per_device(): levels = levels.reshape(1, width)  1.17 us

profile of v2, /device:TPU:1, one launch (start us, length us, event | category | flops | bytes accessed | tf_op | source)
XLA Modules:
  0.0 57.9 jit_solution(7437996936609220968)
XLA Ops:
  0.0 1.2 %multiply_bitcast_fusion.table = f32[1,128]{1,0:T(1,128)} fusion(f32[16]{0:T(128)} %param.9), kind=kLoop, calls=%fused_computation | loop fusion | flops 128 | bytes 576 | tf_op jit(solution)/shard_map/reshape | solution.py:272
  1.2 54.9 %tile_update.1 = f32[128,1024]{1,0:T(8,128)} custom-call(f32[1024,1024]{1,0:T(8,128)} %perturb.1, bf16[128,1024]{1,0:T(8,128)(2,1)} %observed.1, bf16[128,1024]{1,0:T(8,128)(2,1)} %solved.1, s32[1024,896]{1,0:T(8,128)} %taper_index.1, f32[1,128]{1,0:T(1,128)} %multiply_bitcast_fusion.table), custom_call_target="tpu_custom_call" | custom-call | tf_op jit(solution)/shard_map/tile_update/pallas_call | solution.py:275
  56.0 1.9 %copy.7 = f32[128,1024]{1,0:T(8,128)} copy(f32[128,1024]{1,0:T(8,128)} %tile_update.1) | data formatting | bytes 1048576

commit v3 on v2

--- a/solution.py
+++ b/solution.py
@@ -11,7 +11,8 @@
 MESH = pl.DeviceIdType.MESH
 BF16, F32 = jnp.bfloat16, jnp.float32
 SLOTS = 7
-CUTS = 2
+CUTS = 4
+LEAD = 3
 TILE = 256
 PARTS = 4
 OUTER = (0, 1, 2, 3, -3, -2, -1)
@@ -68,12 +69,12 @@
     for peer in peers:
         pl.semaphore_signal(barrier, inc=1, device_id=peer, device_id_type=MESH)
     own_obs.start()
+    for c in range(PARTS):
+        own_sol[c].start()
     for i in range(4):
         loads[i].start()
     for slot in (0, 1, 4, 2, 3, 5, 6):
         index_loads[slot].start()
-    for c in range(PARTS):
-        own_sol[c].start()
     pl.semaphore_wait(barrier, len(peers))
 
     def remote(src, dst, send, recv, peer):
@@ -90,7 +91,7 @@
 
     def sol_copy(slot, c):
         source, peer = routes[slot]
-        src = solved.at[:, pl.ds(c * span, span)] if source == 0 else sol.at[c, pl.ds(source * width, width)]
+        src = sol.at[c, pl.ds(source * width, width)]
         return remote(src, sol.at[c, pl.ds(slot * width, width)], sol_send.at[slot, c], sol_recv.at[slot, c], peer)
 
     obs_copies = {(slot, i): obs_copy(slot, i) for slot in routes for i in range(CUTS)}
@@ -100,15 +101,23 @@
         for slot in (2, 4, 1):
             obs_copies[slot, i].start()
     for c in range(PARTS):
+        own_sol[c].wait()
         sol_copies[2, c].start()
+
+    levels = [table[i] * (1.0 / (members - 1)) for i in range(table.shape[0])]
 
     def find_rho(slot):
         index_loads[slot].wait()
-        values = jnp.broadcast_to(table[...], (64, width))
 
         def body(i, carry):
             run = pl.ds(pl.multiple_of(i * 64, 64), 64)
-            rho[run, slot * width : (slot + 1) * width] = jnp.take_along_axis(values, index[slot, run, :], axis=1)
+            at = index[slot, run, :]
+            values, bit = levels, 1
+            while len(values) > 1:
+                odd = (at & bit) != 0
+                values = [jnp.where(odd, values[k + 1], values[k]) for k in range(0, len(values), 2)]
+                bit *= 2
+            rho[run, slot * width : (slot + 1) * width] = values[0]
             return carry
 
         lax.fori_loop(0, rows // 64, body, 0)
@@ -155,33 +164,37 @@
             if source == slot_from:
                 sol_copies[slot, c].start()
 
+    def sol_step(c):
+        send_sol(c)
+        pass_sol(2, c)
+
     find_rho(0)
     find_rho(1)
     own_obs.wait()
     obs_came(1)
     weigh(0, 2)
-    pass_obs(2, 0)
+    for i in range(CUTS // 2):
+        pass_obs(2, i)
     find_rho(4)
     obs_came(4)
     weigh(4, 1)
-    pass_obs(2, 1)
-    send_sol(0)
+    for i in range(CUTS // 2, CUTS):
+        pass_obs(2, i)
     find_rho(2)
     find_rho(3)
     obs_came(3)
     weigh(2, 2)
-    pass_sol(2, 0)
-    send_sol(1)
+    sol_step(0)
     find_rho(5)
     find_rho(6)
-    pass_obs(5, 0)
-    pass_sol(2, 1)
-    send_sol(2)
-    pass_obs(5, 1)
+    for i in range(CUTS - 1):
+        pass_obs(5, i)
+    sol_step(1)
+    pass_obs(5, CUTS - 1)
     obs_came(6)
     weigh(5, 2)
-    pass_sol(2, 2)
-    send_sol(3)
+    for c in range(2, LEAD):
+        sol_step(c)
 
     def rows_of(half, where):
         return pl.ds(pl.multiple_of((half * ring + where) * share, share), share)
@@ -239,15 +252,14 @@
 
     for c in range(PARTS):
         pass_sol(5, c)
-        own_sol[c].wait()
         for slot in (1, 3, 4, 6):
             sol_copies[slot, c].wait_recv()
         increments(c)
         for k in range(2):
             for w in range(2):
                 y_copies[c, w, k].start()
-        if c == 0:
-            pass_sol(2, 3)
+        if c + LEAD < PARTS:
+            sol_step(c + LEAD)
         if c >= 1:
             join(c - 1)
         if c >= 2:
@@ -268,14 +280,12 @@
     width = observed.shape[0]
     ring = lax.axis_size("y")
     share, span = rows // (2 * ring), members // PARTS
-    levels = jnp.pad(taper_table, (0, width - taper_table.shape[0])) / (members - 1)
-    levels = levels.reshape(1, width)
     anywhere = pl.BlockSpec(memory_space=pl.ANY)
     dma = pltpu.SemaphoreType.DMA
     return pl.pallas_call(
         kernel,
         out_shape=jax.ShapeDtypeStruct((share, members), F32),
-        in_specs=[anywhere] * 4 + [pl.BlockSpec(memory_space=pltpu.VMEM)],
+        in_specs=[anywhere] * 4 + [pl.BlockSpec(memory_space=pltpu.SMEM)],
         out_specs=anywhere,
         scratch_shapes=[
             pltpu.VMEM((rows, members), F32),
@@ -308,10 +318,10 @@
             dma((PARTS,)),
         ],
         compiler_params=pltpu.CompilerParams(
-            collective_id=0, has_side_effects=True, vmem_limit_bytes=67_000_000
+            collective_id=0, has_side_effects=True, vmem_limit_bytes=50_000_000
         ),
         name="tile_update",
-    )(perturb, observed, solved, taper_index, levels)
+    )(*(pltpu.with_memory_space_constraint(a, pltpu.HBM) for a in (perturb, observed, solved, taper_index, taper_table)))
 
 
 AXES = ("z", "xl", "core", "xh", "y")

time: 58.1 us -> 54 us (0.929)
  Pallas kernels: 54.9 us -> 53.1 us
  other arithmetic: 1.17 us -> 0 us
  local copies, waits for them, and re-layouts: 1.89 us -> 0.8 us
    pallas_call x1, Pallas kernels: 54.9 us -> 53.1 us  [per_device(): pl.pallas_call(kernel, out_shape=jax.ShapeDtypeStruct((share, members), F...]
    reshape x1 -> x0, other arithmetic: 1.17 us -> none  [per_device(): levels = levels.reshape(1, width)]
    unnamed x1, local copies, waits for them, and re-layouts: 1.89 us -> 0.8 us
where the time goes in v3:
time: 54 us; the launch traced here: 53.9 us
  Pallas kernels  53.1 us (98%)
  local copies, waits for them, and re-layouts  0.8 us (1%)
    pallas_call x1, Pallas kernels, per_device(): pl.pallas_call(kernel, out_shape=jax.ShapeDtypeStruct((share, members), F...  53.1 us

profile of v3, /device:TPU:1, one launch (start us, length us, event | category | flops | bytes accessed | tf_op | source)
XLA Modules:
  0.0 53.9 jit_solution(2078613623897561502)
XLA Ops:
  0.0 53.1 %tile_update.1 = f32[128,1024]{1,0:T(8,128)S(1)} custom-call(f32[1024,1024]{1,0:T(8,128)} %perturb.1, bf16[128,1024]{1,0:T(8,128)(2,1)} %observed.1, bf16[128,1024]{1,0:T(8,128)(2,1)} %solved.1, s32[1024,896]{1,0:T(8,128)} %taper_index.1, f32[16]{0:T(128)} %table.1), custom_call_target="tpu_custom_call" | custom-call | tf_op jit(solution)/shard_map/tile_update/pallas_call | solution.py:285
  53.1 0.8 %copy.7 = f32[128,1024]{1,0:T(8,128)} copy(f32[128,1024]{1,0:T(8,128)S(1)} %tile_update.1) | data formatting | bytes 1048576

commit v4 on v3

--- a/solution.py
+++ b/solution.py
@@ -12,6 +12,7 @@
 BF16, F32 = jnp.bfloat16, jnp.float32
 SLOTS = 7
 CUTS = 4
+RING_FIRST, ACROSS_FIRST = (1, 3), (0, 2)
 LEAD = 3
 TILE = 256
 PARTS = 4
@@ -22,8 +23,10 @@
 def kernel(
     perturb, observed, solved, taper_index, table, out,
     x_full, x_half, obs, sol, index, rho, weighted, part, passed, joined, came, half_out, half_in, half_own, result,
+    cross_in, cross_sum, ring_in,
     load_sem, obs_load_sem, sol_load_sem, index_sem, out_sem,
     obs_send, obs_recv, sol_send, sol_recv, y_send, y_recv, x_send, x_recv,
+    cross_send, cross_recv, ring_send, ring_recv,
 ):
     z, xl, core, xh, y = (lax.axis_index(a) for a in ("z", "xl", "core", "xh", "y"))
     depth, ring = lax.axis_size("z"), lax.axis_size("y")
@@ -65,7 +68,7 @@
         )
 
     barrier = pltpu.get_barrier_semaphore()
-    peers = (mate, across, slant, ahead, behind, {"y": y_up}, {"y": y_down}, opposite)
+    peers = (mate, across, slant, ahead, behind, {"y": y_up}, {"y": y_down}, {"y": far}, opposite)
     for peer in peers:
         pl.semaphore_signal(barrier, inc=1, device_id=peer, device_id_type=MESH)
     own_obs.start()
@@ -209,10 +212,10 @@
             src, dst = joined.at[c, way_y], came.at[c, way_y, way_y]
         return remote(src, dst, y_send.at[c, way_y, kind], y_recv.at[c, way_y, kind], peer)
 
-    y_copies = {(c, w, k): y_copy(c, w, k) for c in range(PARTS) for w in range(2) for k in range(3)}
-    x_copies = [
-        remote(half_out.at[c], half_in.at[c], x_send.at[c], x_recv.at[c], opposite) for c in range(PARTS)
-    ]
+    y_copies = {(c, w, k): y_copy(c, w, k) for c in RING_FIRST for w in range(2) for k in range(3)}
+    x_copies = {
+        c: remote(half_out.at[c], half_in.at[c], x_send.at[c], x_recv.at[c], opposite) for c in RING_FIRST
+    }
     writes = [
         pltpu.make_async_copy(result.at[c], out.at[:, pl.ds(c * span, span)], out_sem.at[c]) for c in range(PARTS)
     ]
@@ -250,26 +253,66 @@
         result[c] = half_own[c] + half_in[c].astype(F32)
         writes[c].start()
 
+    places = {k: lax.rem(y + k, ring) for k in (2, 1, 3, 0)}
+    cross_copies = {
+        (c, k): remote(
+            part.at[c, rows_of(1 - xh, places[k])], cross_in.at[c, k], cross_send.at[c, k], cross_recv.at[c, k], opposite
+        )
+        for c in ACROSS_FIRST
+        for k in places
+    }
+    ring_copies = {
+        (c, k): remote(cross_sum.at[c, k], ring_in.at[c, k], ring_send.at[c, k], ring_recv.at[c, k], {"y": places[k]})
+        for c in ACROSS_FIRST
+        for k in places
+        if k
+    }
+
+    def pass_cross(c):
+        for k in places:
+            cross_copies[c, k].wait_recv()
+            total = part[c, rows_of(xh, places[k]), :].astype(F32) + cross_in[c, k].astype(F32)
+            if k:
+                cross_sum[c, k] = total.astype(BF16)
+                ring_copies[c, k].start()
+            else:
+                half_own[c] = total + x_full[rows_of(xh, y), c * span : (c + 1) * span]
+
+    def finish_cross(c):
+        total = half_own[c]
+        for k in (1, 3, 2):
+            ring_copies[c, k].wait_recv()
+            total = total + ring_in[c, k].astype(F32)
+        result[c] = total
+        writes[c].start()
+
     for c in range(PARTS):
         pass_sol(5, c)
         for slot in (1, 3, 4, 6):
             sol_copies[slot, c].wait_recv()
         increments(c)
-        for k in range(2):
-            for w in range(2):
-                y_copies[c, w, k].start()
+        if c in ACROSS_FIRST:
+            for k in places:
+                cross_copies[c, k].start()
+        else:
+            for k in range(2):
+                for w in range(2):
+                    y_copies[c, w, k].start()
         if c + LEAD < PARTS:
             sol_step(c + LEAD)
-        if c >= 1:
-            join(c - 1)
-        if c >= 2:
-            gather(c - 2)
-    join(PARTS - 1)
-    for c in range(max(PARTS - 2, 0), PARTS):
-        gather(c)
-    for c in range(PARTS):
-        finish(c)
-    for copy in (*obs_copies.values(), *sol_copies.values(), *y_copies.values(), *x_copies):
+        if c == 2:
+            join(1)
+    pass_cross(0)
+    join(3)
+    gather(1)
+    pass_cross(2)
+    gather(3)
+    finish_cross(0)
+    finish(1)
+    finish_cross(2)
+    finish(3)
+    for copy in (*obs_copies.values(), *sol_copies.values(), *y_copies.values(), *x_copies.values(),
+                 *cross_copies.values(), *ring_copies.values()):
         copy.wait_send()
     for copy in writes:
         copy.wait()
@@ -303,6 +346,9 @@
             pltpu.VMEM((PARTS, share, span), BF16),
             pltpu.VMEM((PARTS, share, span), F32),
             pltpu.VMEM((PARTS, share, span), F32),
+            pltpu.VMEM((PARTS, ring, share, span), BF16),
+            pltpu.VMEM((PARTS, ring, share, span), BF16),
+            pltpu.VMEM((PARTS, ring, share, span), BF16),
             dma((4,)),
             dma,
             dma((PARTS,)),
@@ -316,6 +362,10 @@
             dma((PARTS, 2, 3)),
             dma((PARTS,)),
             dma((PARTS,)),
+            dma((PARTS, ring)),
+            dma((PARTS, ring)),
+            dma((PARTS, ring)),
+            dma((PARTS, ring)),
         ],
         compiler_params=pltpu.CompilerParams(
             collective_id=0, has_side_effects=True, vmem_limit_bytes=50_000_000

time: 54 us -> 53.5 us (level)
    pallas_call x1, Pallas kernels: 53.1 us -> 52.6 us  [per_device(): pl.pallas_call(kernel, out_shape=jax.ShapeDtypeStruct((share, members), F...]
where the time goes in v4:
time: 53.5 us; the launch traced here: 53.4 us
  Pallas kernels  52.6 us (98%)
  local copies, waits for them, and re-layouts  0.8 us (1%)
    pallas_call x1, Pallas kernels, per_device(): pl.pallas_call(kernel, out_shape=jax.ShapeDtypeStruct((share, members), F...  52.6 us

profile of v4, /device:TPU:1, one launch (start us, length us, event | category | flops | bytes accessed | tf_op | source)
XLA Modules:
  0.0 53.4 jit_solution(11371397703993661464)
XLA Ops:
  0.0 52.6 %tile_update.1 = f32[128,1024]{1,0:T(8,128)S(1)} custom-call(f32[1024,1024]{1,0:T(8,128)} %perturb.1, bf16[128,1024]{1,0:T(8,128)(2,1)} %observed.1, bf16[128,1024]{1,0:T(8,128)(2,1)} %solved.1, s32[1024,896]{1,0:T(8,128)} %taper_index.1, f32[16]{0:T(128)} %table.1), custom_call_target="tpu_custom_call" | custom-call | tf_op jit(solution)/shard_map/tile_update/pallas_call | solution.py:328
  52.6 0.8 %copy.7 = f32[128,1024]{1,0:T(8,128)} copy(f32[128,1024]{1,0:T(8,128)S(1)} %tile_update.1) | data formatting | bytes 1048576

commit v5 on v4

--- a/solution.py
+++ b/solution.py
@@ -12,7 +12,8 @@
 BF16, F32 = jnp.bfloat16, jnp.float32
 SLOTS = 7
 CUTS = 4
-RING_FIRST, ACROSS_FIRST = (1, 3), (0, 2)
+RING_FIRST, ACROSS_FIRST = (0, 1, 3), (2,)
+TURNS = ((1, 3), (2, 0), (2, 1), (0, 2), (2, 3))
 LEAD = 3
 TILE = 256
 PARTS = 4
@@ -72,11 +73,13 @@
     for peer in peers:
         pl.semaphore_signal(barrier, inc=1, device_id=peer, device_id_type=MESH)
     own_obs.start()
+    for slot in (0, 1):
+        index_loads[slot].start()
+    for i in range(4):
+        loads[i].start()
     for c in range(PARTS):
         own_sol[c].start()
-    for i in range(4):
-        loads[i].start()
-    for slot in (0, 1, 4, 2, 3, 5, 6):
+    for slot in (4, 2, 3, 5, 6):
         index_loads[slot].start()
     pl.semaphore_wait(barrier, len(peers))
 
@@ -103,9 +106,6 @@
     for i in range(CUTS):
         for slot in (2, 4, 1):
             obs_copies[slot, i].start()
-    for c in range(PARTS):
-        own_sol[c].wait()
-        sol_copies[2, c].start()
 
     levels = [table[i] * (1.0 / (members - 1)) for i in range(table.shape[0])]
 
@@ -142,15 +142,6 @@
         for i in range(CUTS):
             obs_copies[slot, i].wait_recv()
 
-    for i in range(4):
-        loads[i].wait()
-
-        def convert(j, carry):
-            run = pl.ds(pl.multiple_of(i * step + j * 16, 16), 16)
-            x_half[run, :] = x_full[run, :].astype(BF16)
-            return carry
-
-        lax.fori_loop(0, step // 16, convert, 0)
     def pass_obs(slot_from, i):
         obs_copies[slot_from, i].wait_recv()
         for slot, (source, _) in routes.items():
@@ -173,27 +164,40 @@
 
     find_rho(0)
     find_rho(1)
+    for i in range(4):
+        loads[i].wait()
+
+        def convert(j, carry):
+            run = pl.ds(pl.multiple_of(i * step + j * 16, 16), 16)
+            x_half[run, :] = x_full[run, :].astype(BF16)
+            return carry
+
+        lax.fori_loop(0, step // 16, convert, 0)
+    for c in range(PARTS):
+        own_sol[c].wait()
+        sol_copies[2, c].start()
     own_obs.wait()
+    pass_obs(2, 0)
     obs_came(1)
     weigh(0, 2)
-    for i in range(CUTS // 2):
-        pass_obs(2, i)
+    pass_obs(2, 1)
     find_rho(4)
     obs_came(4)
     weigh(4, 1)
-    for i in range(CUTS // 2, CUTS):
-        pass_obs(2, i)
+    pass_obs(2, 2)
     find_rho(2)
+    pass_obs(2, 3)
     find_rho(3)
     obs_came(3)
     weigh(2, 2)
     sol_step(0)
+    pass_obs(5, 0)
     find_rho(5)
+    pass_obs(5, 1)
     find_rho(6)
-    for i in range(CUTS - 1):
-        pass_obs(5, i)
+    pass_obs(5, 2)
     sol_step(1)
-    pass_obs(5, CUTS - 1)
+    pass_obs(5, 3)
     obs_came(6)
     weigh(5, 2)
     for c in range(2, LEAD):
@@ -300,17 +304,15 @@
                     y_copies[c, w, k].start()
         if c + LEAD < PARTS:
             sol_step(c + LEAD)
-        if c == 2:
-            join(1)
-    pass_cross(0)
-    join(3)
-    gather(1)
-    pass_cross(2)
-    gather(3)
-    finish_cross(0)
-    finish(1)
-    finish_cross(2)
-    finish(3)
+        if c - 1 in RING_FIRST:
+            join(c - 1)
+    for turn, c in TURNS:
+        (pass_cross, join, gather)[turn](c)
+    for c in range(PARTS):
+        if c in ACROSS_FIRST:
+            finish_cross(c)
+        else:
+            finish(c)
     for copy in (*obs_copies.values(), *sol_copies.values(), *y_copies.values(), *x_copies.values(),
                  *cross_copies.values(), *ring_copies.values()):
         copy.wait_send()

time: 53.5 us -> 51.4 us (0.961)
  the two profiles are of different devices: /device:TPU:1 before, /device:TPU:24 now
where the time goes in v5:
time: 51.4 us
  Pallas kernels  50.6 us (98%)
  local copies, waits for them, and re-layouts  0.8 us (2%)
    pallas_call x1, Pallas kernels, per_device(): pl.pallas_call(kernel, out_shape=jax.ShapeDtypeStruct((share, members), F...  50.6 us

profile of v5, /device:TPU:24, one launch (start us, length us, event | category | flops | bytes accessed | tf_op | source)
XLA Modules:
  0.0 51.4 jit_solution(17027624886192461788)
XLA Ops:
  0.0 50.6 %tile_update.1 = f32[128,1024]{1,0:T(8,128)S(1)} custom-call(f32[1024,1024]{1,0:T(8,128)} %perturb.1, bf16[128,1024]{1,0:T(8,128)(2,1)} %observed.1, bf16[128,1024]{1,0:T(8,128)(2,1)} %solved.1, s32[1024,896]{1,0:T(8,128)} %taper_index.1, f32[16]{0:T(128)} %table.1), custom_call_target="tpu_custom_call" | custom-call | tf_op jit(solution)/shard_map/tile_update/pallas_call | solution.py:330
  50.6 0.8 %copy.7 = f32[128,1024]{1,0:T(8,128)} copy(f32[128,1024]{1,0:T(8,128)S(1)} %tile_update.1) | data formatting | bytes 1048576

commit v6 on v5

--- a/solution.py
+++ b/solution.py
@@ -13,8 +13,8 @@
 SLOTS = 7
 CUTS = 4
 RING_FIRST, ACROSS_FIRST = (0, 1, 3), (2,)
-TURNS = ((1, 3), (2, 0), (2, 1), (0, 2), (2, 3))
-LEAD = 3
+TURNS = ((1, 3), (2, 0), (0, 2), (2, 1), (2, 3))
+LEAD = 2
 TILE = 256
 PARTS = 4
 OUTER = (0, 1, 2, 3, -3, -2, -1)

time: 51.4 us -> 51.1 us (level)
  the two profiles are of different devices: /device:TPU:24 before, /device:TPU:1 now
where the time goes in v6:
time: 51.1 us; the launch traced here: 51 us
  Pallas kernels  50.2 us (98%)
  local copies, waits for them, and re-layouts  0.8 us (2%)
    pallas_call x1, Pallas kernels, per_device(): pl.pallas_call(kernel, out_shape=jax.ShapeDtypeStruct((share, members), F...  50.2 us

profile of v6, /device:TPU:1, one launch (start us, length us, event | category | flops | bytes accessed | tf_op | source)
XLA Modules:
  0.0 51.0 jit_solution(3442607868832121732)
XLA Ops:
  0.0 50.2 %tile_update.1 = f32[128,1024]{1,0:T(8,128)S(1)} custom-call(f32[1024,1024]{1,0:T(8,128)} %perturb.1, bf16[128,1024]{1,0:T(8,128)(2,1)} %observed.1, bf16[128,1024]{1,0:T(8,128)(2,1)} %solved.1, s32[1024,896]{1,0:T(8,128)} %taper_index.1, f32[16]{0:T(128)} %table.1), custom_call_target="tpu_custom_call" | custom-call | tf_op jit(solution)/shard_map/tile_update/pallas_call | solution.py:330
  50.2 0.8 %copy.7 = f32[128,1024]{1,0:T(8,128)} copy(f32[128,1024]{1,0:T(8,128)S(1)} %tile_update.1) | data formatting | bytes 1048576
